TPU v7x, 512 devices: a whole 4x4x16 slice. The times are simulated.
512 devices in a mesh: dp: 64 (over y_lo, z, core), blk: 8 (over y_hi, x).
Axes of the slice: x: 4, y: 4 (y_hi: 2, y_lo: 2; y = y_hi * 2 + y_lo), z: 16, core: 2. Of those that a mesh axis runs over, the one named last changes fastest.
Arguments:
- resid: bfloat16 [2048, 2048], P('dp'), may hold values from -40 to 40
- queries: bfloat16 [2048, 16, 128], P('dp', 'blk'), may hold values from -60 to 60
- new_kv: bfloat16 [2048, 2, 8, 128], P('dp', None, 'blk'), may hold values from -6 to 6
- prefix_pool: bfloat16 [2048, 128, 2, 8, 128], P('dp', None, None, 'blk'), may hold values from -6 to 6
- page_table: int32 [64, 32], P('dp'), may hold values from 0 to 31, each once within a row
- prompt_len: int32 [64], P('dp'), may hold values from 1 to 4096, 131072 in all
- tail_pool: bfloat16 [1024, 128, 2, 8, 128], P('dp', None, None, 'blk'), may hold values from -6 to 6
- tail_len: int32 [64, 16], P('dp'), may hold values from 1 to 128, 1024 in all within a row
- migration: int32 [1024], replicated, may hold values from 0 to 1023, each once
- out_w: bfloat16 [2048, 2048], P('blk'), may hold values from -0.125 to 0.125
- mlp_gain: bfloat16 [2048], replicated, may hold values from 0.099609375 to 1.8984375
- gate_w: bfloat16 [2048, 6144], P('blk', 'dp'), may hold values from -0.125 to 0.125
- up_w: bfloat16 [2048, 6144], P('blk', 'dp'), may hold values from -0.125 to 0.125
- down_w: bfloat16 [6144, 2048], P('dp', 'blk'), may hold values from -0.078125 to 0.078125
- final_gain: bfloat16 [2048], P('blk'), may hold values from 0.099609375 to 1.8984375
- score_w: bfloat16 [2048], P('blk'), may hold values from -0.125 to 0.125
Outputs:
- hidden_out: bfloat16 [2048, 2048], P('dp', 'blk')
- score: float32 [2048], P('dp')
Inputs may be any that keep to these rules, and one draw needn't show every extreme that they name: `page_table`: each row lists every page of the device's pool once. `migration`: names every continuation once.
All inputs are finite; a program needn't handle non-finite values. No bound on the sum of `prompt_len` on one device may be relied on, other than what follows from the above.
Results may differ from a plain program's by a relative error of at most 0.012.
Values may be sent and summed in bfloat16 or wider, within the bound.
A program may use at most 64 MiB of HBM per device.

v0:
```python
import math
import jax
import jax.numpy as jnp
from jax import lax
from jax.sharding import PartitionSpec as P

D = 2048
NEW = 2
NEG = -1e30
EPS = 1e-06


def attend_prompt(queries, pool, table, prompt_len, tails, tail_len, pairs):
    token_rows, heads, width = queries.shape
    groups = pairs.shape[2]
    repeat = heads // groups
    conts = tails.shape[0]
    fresh = token_rows // conts
    prefix = jnp.take(pool, table, axis=0).reshape(-1, 2, groups, width)
    span = prefix.shape[0]
    grouped = queries.reshape(conts, fresh, groups, repeat, width)
    recent = pairs.reshape(conts, fresh, 2, groups, width)
    factor = 1.0 / math.sqrt(width)
    pre_scores = (
        jnp.einsum("cngrd,pgd->gcnrp", grouped, prefix[:, 0], preferred_element_type=jnp.float32)
        * factor
    )
    tail_scores = (
        jnp.einsum("cngrd,ctgd->gcnrt", grouped, tails[:, :, 0], preferred_element_type=jnp.float32)
        * factor
    )
    new_scores = (
        jnp.einsum(
            "cngrd,cmgd->gcnrm", grouped, recent[:, :, 0], preferred_element_type=jnp.float32
        )
        * factor
    )
    pre_mask = (jnp.arange(span) < prompt_len)[None, None, None, None, :]
    tail_mask = (jnp.arange(tails.shape[1])[None, :] < tail_len[:, None])[None, :, None, None, :]
    new_mask = (jnp.arange(fresh)[None, :] <= jnp.arange(fresh)[:, None])[None, None, :, None, :]
    pre_scores = jnp.where(pre_mask, pre_scores, NEG)
    tail_scores = jnp.where(tail_mask, tail_scores, NEG)
    new_scores = jnp.where(new_mask, new_scores, NEG)
    highest = jnp.maximum(
        jnp.maximum(jnp.max(pre_scores, -1), jnp.max(tail_scores, -1)), jnp.max(new_scores, -1)
    )[..., None]
    pre_weights = jnp.where(pre_mask, jnp.exp(pre_scores - highest), 0.0)
    tail_weights = jnp.where(tail_mask, jnp.exp(tail_scores - highest), 0.0)
    new_weights = jnp.where(new_mask, jnp.exp(new_scores - highest), 0.0)
    total = jnp.sum(pre_weights, -1) + jnp.sum(tail_weights, -1) + jnp.sum(new_weights, -1)
    mixed = jnp.einsum(
        "gcnrp,pgd->cngrd",
        pre_weights.astype(jnp.bfloat16),
        prefix[:, 1],
        preferred_element_type=jnp.float32,
    )
    mixed = mixed + jnp.einsum(
        "gcnrt,ctgd->cngrd",
        tail_weights.astype(jnp.bfloat16),
        tails[:, :, 1],
        preferred_element_type=jnp.float32,
    )
    mixed = mixed + jnp.einsum(
        "gcnrm,cmgd->cngrd",
        new_weights.astype(jnp.bfloat16),
        recent[:, :, 1],
        preferred_element_type=jnp.float32,
    )
    mixed = mixed / jnp.transpose(total, (1, 2, 0, 3))[..., None]
    return mixed.reshape(token_rows, heads * width).astype(jnp.bfloat16)


def shards(
    resid,
    queries,
    new_kv,
    prefix_pool,
    page_table,
    prompt_len,
    tail_pool,
    tail_len,
    migration,
    out_w,
    mlp_gain,
    gate_w,
    up_w,
    down_w,
    final_gain,
    score_w,
):
    token_rows = resid.shape[0]
    attn = attend_prompt(
        queries, prefix_pool, page_table[0], prompt_len[0], tail_pool, tail_len[0], new_kv
    )
    partial_value = jnp.dot(attn, out_w, preferred_element_type=jnp.float32)
    mixed = lax.psum(partial_value.astype(jnp.bfloat16), "blk").astype(jnp.float32)
    middle = resid.astype(jnp.float32) + mixed
    normed = (
        middle
        * lax.rsqrt(jnp.mean(middle * middle, -1, keepdims=True) + EPS)
        * mlp_gain.astype(jnp.float32)
    ).astype(jnp.bfloat16)
    feat_width = gate_w.shape[0]
    units = gate_w.shape[1]
    block_index = lax.axis_index("blk")
    home_index = lax.axis_index("dp")
    feat_slice = lax.dynamic_slice_in_dim(normed, block_index * feat_width, feat_width, 1)
    middle_slice = lax.dynamic_slice_in_dim(middle, block_index * feat_width, feat_width, 1)
    piece = lax.all_gather(feat_slice, "dp", axis=0, tiled=True)
    partial_units = jnp.concatenate(
        [
            jnp.dot(piece, gate_w, preferred_element_type=jnp.float32),
            jnp.dot(piece, up_w, preferred_element_type=jnp.float32),
        ],
        axis=1,
    )
    summed = lax.psum(partial_units.astype(jnp.bfloat16), "blk").astype(jnp.float32)
    hidden = (jax.nn.silu(summed[:, :units]) * summed[:, units:]).astype(jnp.bfloat16)
    source = (migration[:, None] * NEW + jnp.arange(NEW, dtype=jnp.int32)[None, :]).reshape(-1)
    term = jnp.dot(jnp.take(hidden, source, axis=0), down_w, preferred_element_type=jnp.float32)
    local_rows = source - home_index * token_rows
    own_rows = (local_rows >= 0) & (local_rows < token_rows)
    carried = jnp.take(middle_slice, jnp.clip(local_rows, 0, token_rows - 1), axis=0)
    moved = lax.psum_scatter(
        term + jnp.where(own_rows[:, None], carried, 0.0), "dp", scatter_dimension=0, tiled=True
    )
    weighted = final_gain.astype(jnp.float32) * score_w.astype(jnp.float32)
    squares, terms = lax.psum((jnp.sum(moved * moved, -1), jnp.sum(moved * weighted, -1)), "blk")
    score = terms * lax.rsqrt(squares / D + EPS)
    return (moved.astype(jnp.bfloat16), score)


def solution(mesh):
    return jax.shard_map(
        shards,
        mesh=mesh,
        in_specs=(
            P("dp", None),
            P("dp", "blk", None),
            P("dp", None, "blk", None),
            P("dp", None, None, "blk", None),
            P("dp", None),
            P("dp"),
            P("dp", None, None, "blk", None),
            P("dp", None),
            P(),
            P("blk", None),
            P(),
            P("blk", "dp"),
            P("blk", "dp"),
            P("dp", "blk"),
            P("blk"),
            P("blk"),
        ),
        out_specs=(P("dp", "blk"), P("dp")),
        check_vma=False,
    )
```

profile of v0, /device:TPU:8, one launch (start us, length us, event | category | flops | bytes accessed | tf_op | source)
XLA Modules:
  0.0 631.7 jit_solution(11279439814743314583)
XLA Ops:
  7.2 0.8 fusion.25
  9.4 6.2 gather_fusion
  15.5 3.6 copy.69
  19.3 2.3 fusion.31
  22.7 2.0 broadcast_select_fusion
  24.7 1.3 copy-done.2
  27.9 1.6 fusion.11
  29.8 2.0 fusion.6
  31.9 0.9 convolution_convert_fusion.2
  32.9 0.8 dynamic-slice
  33.6 102.1 %all-reduce.4.cloned.1.call-done = bf16[32,2048]{1,0:T(8,128)(2,1)} async-done(((bf16[32,2048]{1,0:T(8,128)(2,1)}), bf16[32,2048]{1,0:T(8,128)(2,1)}) %all-reduce.4.cloned.1.call-update) | async-done | bytes 131088 | tf_op jit(solution)/shard_map/psum | solution.py:96
  135.7 1.1 convert_add_fusion
  138.4 119.5 %all-gather.2.cloned.1.call-done = bf16[2048,256]{1,0:T(8,128)(2,1)} async-done(((bf16[32,256]{1,0:T(8,128)(2,1)}), bf16[2048,256]{1,0:T(8,128)(2,1)}) %all-gather.2.cloned.1.call-update) | async-done | bytes 1048592 | tf_op jit(solution)/shard_map/all_gather | solution.py:109
  257.9 1.7 convolution_convert_fusion
  259.6 1.7 convolution_convert_fusion.1
  261.3 0.9 pad_maximum_fusion
  262.4 8.6 %gather_fusion.2 = f32[2048,256]{1,0:T(8,128)} fusion(f32[32,256]{1,0:T(8,128)S(1)} %get-tuple-element.7, s32[2048]{0:T(1024)S(1)} %broadcast_clamp_fusion), kind=kCustom, calls=%fused_computation.2 | custom fusion | bytes 4202496 | tf_op jit(solution)/shard_map/jit(_take)/gather | solution.py:123
  270.9 89.1 %all-reduce.6.cloned.1.call-done = bf16[2048,192]{0,1:T(8,128)(2,1)} async-done(((bf16[2048,192]{0,1:T(8,128)(2,1)}), bf16[2048,192]{0,1:T(8,128)(2,1)}) %all-reduce.6.cloned.1.call-update) | async-done | bytes 786448 | tf_op jit(solution)/shard_map/psum | solution.py:117
  360.0 1.3 convert_element_type.59
  361.9 6.2 gather_fusion.1
  368.1 4.9 convolution_add_fusion
  373.6 226.0 %reduce-scatter.2.cloned.1.call-done = f32[32,256]{1,0:T(8,128)} async-done(((f32[2048,256]{1,0:T(8,128)}), f32[32,256]{1,0:T(8,128)}) %reduce-scatter.2.cloned.1.call-update) | async-done | bytes 32784 | tf_op jit(solution)/shard_map/reduce_scatter | solution.py:124
  599.6 1.5 multiply_reduce_fusion.1
  601.1 23.5 %all-reduce = (f32[32]{0:T(128)S(1)}, f32[32]{0:T(128)S(1)}) all-reduce(f32[32]{0:T(128)S(1)} %get-tuple-element.3, f32[32]{0:T(128)S(1)} %get-tuple-element.2), channel_id=1, replica_groups=mesh['dp'=64,'blk'=8] {'blk'}, use_global_device_ids=true, to_apply=%region_11.12 | all-reduce | flops 64 | bytes 512 | tf_op jit(solution)/shard_map/psum | solution.py:128
  (74 shorter events, 7.5 us)
Async XLA Ops:
  7.2 2.2 copy-start
  7.2 128.6 %all-reduce.4.cloned.1.call-start = ((), (), s32[]{:S(2)}) async-start(), calls=%async_computation.1 | async-start | bytes 262144 | tf_op jit(solution)/shard_map/psum | solution.py:96
  15.5 3.7 copy-start.11
  15.5 3.7 copy-start.1
  19.3 2.3 copy-start.14
  19.3 2.9 copy-start.9
  24.7 1.4 copy-start.2
  26.6 1.0 copy-start.4
  27.9 3.9 copy-start.3
  29.8 105.9 %copy-start.5 = (bf16[32,2048]{1,0:T(8,128)(2,1)S(1)}, bf16[32,2048]{1,0:T(8,128)(2,1)}, u32[]{:S(2)}) copy-start(bf16[32,2048]{1,0:T(8,128)(2,1)} %param.16) | copy-start | bytes 393220
  29.8 107.7 %copy-start.10 = (s32[1024]{0:T(1024)S(1)}, s32[1024]{0:T(1024)}, u32[]{:S(2)}) copy-start(s32[1024]{0:T(1024)} %param.24) | copy-start | bytes 12292
  31.8 226.1 %copy-start.7 = (bf16[256,96]{0,1:T(8,128)(2,1)S(1)}, bf16[256,96]{0,1:T(8,128)(2,1)}, u32[]{:S(2)}) copy-start(bf16[256,96]{0,1:T(8,128)(2,1)} %param.28) | copy-start | bytes 147460
  32.8 226.8 %copy-start.8 = (bf16[256,96]{0,1:T(8,128)(2,1)S(1)}, bf16[256,96]{0,1:T(8,128)(2,1)}, u32[]{:S(2)}) copy-start(bf16[256,96]{0,1:T(8,128)(2,1)} %param.27) | copy-start | bytes 147460
  32.8 225.1 %all-gather.2.cloned.1.call-start = ((), (), s32[]{:S(2)}) async-start(), calls=%async_computation.2 | async-start | bytes 1064960 | tf_op jit(solution)/shard_map/all_gather | solution.py:109
  137.5 222.5 %all-reduce.6.cloned.1.call-start = ((), (), s32[]{:S(2)}) async-start(), calls=%async_computation.3 | async-start | bytes 1572864 | tf_op jit(solution)/shard_map/psum | solution.py:117
  262.2 337.3 %reduce-scatter.2.cloned.1.call-start = ((), (), s32[]{:S(2)}) async-start(), calls=%async_computation.4 | async-start | bytes 2129920 | tf_op jit(solution)/shard_map/reduce_scatter | solution.py:124
  361.8 6.2 copy-start.6
  372.9 0.7 copy-start.12
  372.9 0.7 copy-start.13
Sparse Core Ops, SparseCore 0:
  32.9 102.7 all-reduce.3
  138.7 119.1 all-gather.1
  262.4 97.6 all-reduce.5
  373.1 226.4 reduce-scatter.1
where the time goes:
time: 632 us
  waiting for transfers between devices  537 us (85%)
  local copies, waits for them, and re-layouts  31.4 us (5%)
  blocking collectives  23.5 us (4%)
  between operations  14.7 us (2%)
  matrix products  14.3 us (2%)
  other arithmetic  10.8 us (2%)
    reduce_scatter x1, waiting for transfers between devices, shards(): lax.psum_scatter(term + jnp.where(own_rows[:, None], carried, 0.0), 'dp',...  226 us
    all_gather x1, waiting for transfers between devices, shards(): piece = lax.all_gather(feat_slice, 'dp', axis=0, tiled=True)  120 us
    psum x1, waiting for transfers between devices, shards(): lax.psum(partial_value.astype(jnp.bfloat16), 'blk').astype(jnp.float32)  102 us
    psum x1, waiting for transfers between devices, shards(): lax.psum(partial_units.astype(jnp.bfloat16), 'blk').astype(jnp.float32)  89.1 us
    psum x1, blocking collectives, shards(): lax.psum((jnp.sum(moved * moved, -1), jnp.sum(moved * weighted, -1)), 'blk')  23.5 us
  transfers between devices with their start and end apart: 4, of which 4 were waited for; matrix products, arithmetic and copies ran while one was open for 2% of the time, Pallas kernels for 0%

commit v1 on v0

--- a/solution.py
+++ b/solution.py
@@ -8,6 +8,11 @@
 NEW = 2
 NEG = -1e30
 EPS = 1e-06
+
+
+def summed_here(value, mesh_axis):
+    pieces = lax.all_gather(value, mesh_axis)
+    return jnp.sum(pieces, axis=0)
 
 
 def attend_prompt(queries, pool, table, prompt_len, tails, tail_len, pairs):
@@ -114,7 +119,7 @@
         ],
         axis=1,
     )
-    summed = lax.psum(partial_units.astype(jnp.bfloat16), "blk").astype(jnp.float32)
+    summed = summed_here(partial_units.astype(jnp.bfloat16), "blk").astype(jnp.float32)
     hidden = (jax.nn.silu(summed[:, :units]) * summed[:, units:]).astype(jnp.bfloat16)
     source = (migration[:, None] * NEW + jnp.arange(NEW, dtype=jnp.int32)[None, :]).reshape(-1)
     term = jnp.dot(jnp.take(hidden, source, axis=0), down_w, preferred_element_type=jnp.float32)

time: 632 us -> 641 us (1.014)
    all_gather x0 -> x1, waiting for transfers between devices: none -> 91.5 us  [summed_here(): pieces = lax.all_gather(value, mesh_axis)]
    psum x1 -> x0, waiting for transfers between devices: 89.1 us -> none  [shards(): lax.psum(partial_units.astype(jnp.bfloat16), 'blk').astype(jnp.float32)]
where the time goes in v1:
time: 641 us; the launch traced here: 640 us
  waiting for transfers between devices  540 us (84%)
  local copies, waits for them, and re-layouts  32.6 us (5%)
  blocking collectives  23.5 us (4%)
  other arithmetic  15 us (2%)
  between operations  14.7 us (2%)
  matrix products  14.3 us (2%)
    reduce_scatter x1, waiting for transfers between devices, shards(): lax.psum_scatter(term + jnp.where(own_rows[:, None], carried, 0.0), 'dp',...  226 us
    all_gather x1, waiting for transfers between devices, shards(): piece = lax.all_gather(feat_slice, 'dp', axis=0, tiled=True)  120 us
    psum x1, waiting for transfers between devices, shards(): lax.psum(partial_value.astype(jnp.bfloat16), 'blk').astype(jnp.float32)  102 us
    all_gather x1, waiting for transfers between devices, summed_here(): pieces = lax.all_gather(value, mesh_axis)  91.5 us
    psum x1, blocking collectives, shards(): lax.psum((jnp.sum(moved * moved, -1), jnp.sum(moved * weighted, -1)), 'blk')  23.5 us
  transfers between devices with their start and end apart: 4, of which 4 were waited for; matrix products, arithmetic and copies ran while one was open for 2% of the time, Pallas kernels for 0%

profile of v1, /device:TPU:8, one launch (start us, length us, event | category | flops | bytes accessed | tf_op | source)
XLA Modules:
  0.0 640.1 jit_solution(4874431722663508482)
XLA Ops:
  7.2 0.8 fusion.27
  9.4 6.2 gather_fusion
  15.5 3.6 copy.67
  19.3 2.3 fusion.33
  22.7 2.0 broadcast_select_fusion
  24.7 1.3 copy-done.2
  27.9 1.6 fusion.13
  29.8 2.0 fusion.8
  31.9 0.9 convolution_convert_fusion.2
  33.6 102.1 %all-reduce.3.cloned.1.call-done = bf16[32,2048]{1,0:T(8,128)(2,1)} async-done(((bf16[32,2048]{1,0:T(8,128)(2,1)}), bf16[32,2048]{1,0:T(8,128)(2,1)}) %all-reduce.3.cloned.1.call-update) | async-done | bytes 131088 | tf_op jit(solution)/shard_map/psum | solution.py:101
  135.7 1.1 convert_add_fusion
  137.6 120.4 %all-gather.3.cloned.1.call-done = bf16[2048,256]{1,0:T(8,128)(2,1)} async-done(((bf16[32,256]{1,0:T(8,128)(2,1)}), bf16[2048,256]{1,0:T(8,128)(2,1)}) %all-gather.3.cloned.1.call-update) | async-done | bytes 1048592 | tf_op jit(solution)/shard_map/all_gather | solution.py:114
  257.9 1.7 fusion.2
  259.6 1.7 fusion.3
  261.3 1.0 pad_maximum_fusion
  263.3 8.6 %gather_fusion.2 = f32[2048,256]{1,0:T(8,128)} fusion(f32[32,256]{1,0:T(8,128)S(1)} %get-tuple-element.7, s32[2048]{0:T(1024)S(1)} %broadcast_clamp_fusion), kind=kCustom, calls=%fused_computation.2 | custom fusion | bytes 4202496 | tf_op jit(solution)/shard_map/jit(_take)/gather | solution.py:128
  271.8 91.5 %all-gather.5.cloned.1.call-done = bf16[8,2048,192]{1,2,0:T(8,128)(2,1)} async-done(((bf16[1,2048,192]{1,2,0:T(8,128)(2,1)}), bf16[8,2048,192]{1,2,0:T(8,128)(2,1)}) %all-gather.5.cloned.1.call-update) | async-done | bytes 6291472 | tf_op jit(solution)/shard_map/all_gather | solution.py:14
  363.4 5.1 reduce_sum.70
  368.5 1.4 copy.84
  370.5 6.2 gather_fusion.1
  376.7 4.9 convolution_add_fusion
  382.2 225.8 %reduce-scatter.2.cloned.1.call-done = f32[32,256]{1,0:T(8,128)} async-done(((f32[2048,256]{1,0:T(8,128)}), f32[32,256]{1,0:T(8,128)}) %reduce-scatter.2.cloned.1.call-update) | async-done | bytes 32784 | tf_op jit(solution)/shard_map/reduce_scatter | solution.py:129
  608.0 1.5 multiply_reduce_fusion.1
  609.6 23.5 %all-reduce = (f32[32]{0:T(128)S(1)}, f32[32]{0:T(128)S(1)}) all-reduce(f32[32]{0:T(128)S(1)} %get-tuple-element.3, f32[32]{0:T(128)S(1)} %get-tuple-element.2), channel_id=1, replica_groups=mesh['dp'=64,'blk'=8] {'blk'}, use_global_device_ids=true, to_apply=%region_11.12 | all-reduce | flops 64 | bytes 512 | tf_op jit(solution)/shard_map/psum | solution.py:133
  (75 shorter events, 8.3 us)
Async XLA Ops:
  7.2 2.2 copy-start
  7.2 128.5 %all-reduce.3.cloned.1.call-start = ((), (), s32[]{:S(2)}) async-start(), calls=%async_computation.1 | async-start | bytes 262144 | tf_op jit(solution)/shard_map/psum | solution.py:101
  15.5 3.7 copy-start.11
  15.5 3.7 copy-start.1
  19.3 2.3 copy-start.14
  19.3 2.9 copy-start.9
  24.7 1.4 copy-start.2
  26.6 1.0 copy-start.4
  27.9 3.9 copy-start.3
  29.8 105.9 %copy-start.5 = (bf16[32,2048]{1,0:T(8,128)(2,1)S(1)}, bf16[32,2048]{1,0:T(8,128)(2,1)}, u32[]{:S(2)}) copy-start(bf16[32,2048]{1,0:T(8,128)(2,1)} %param.16) | copy-start | bytes 393220
  29.8 228.1 %copy-start.7 = (bf16[256,96]{0,1:T(8,128)(2,1)S(1)}, bf16[256,96]{0,1:T(8,128)(2,1)}, u32[]{:S(2)}) copy-start(bf16[256,96]{0,1:T(8,128)(2,1)} %param.27) | copy-start | bytes 147460
  31.8 227.8 %copy-start.8 = (bf16[256,96]{0,1:T(8,128)(2,1)S(1)}, bf16[256,96]{0,1:T(8,128)(2,1)}, u32[]{:S(2)}) copy-start(bf16[256,96]{0,1:T(8,128)(2,1)} %param.28) | copy-start | bytes 147460
  32.8 225.1 %all-gather.3.cloned.1.call-start = ((), (), s32[]{:S(2)}) async-start(), calls=%async_computation.2 | async-start | bytes 1064960 | tf_op jit(solution)/shard_map/all_gather | solution.py:114
  137.5 225.9 %all-gather.5.cloned.1.call-start = ((), (), s32[]{:S(2)}) async-start(), calls=%async_computation.3 | async-start | bytes 7077888 | tf_op jit(solution)/shard_map/all_gather | solution.py:14
  259.6 2.8 copy-start.10
  262.3 345.7 %reduce-scatter.2.cloned.1.call-start = ((), (), s32[]{:S(2)}) async-start(), calls=%async_computation.4 | async-start | bytes 2129920 | tf_op jit(solution)/shard_map/reduce_scatter | solution.py:129
  370.4 6.2 copy-start.6
  381.5 0.7 copy-start.12
  381.5 0.7 copy-start.13
Sparse Core Ops, SparseCore 0:
  32.9 102.7 all-reduce.2
  138.7 119.1 all-gather.2
  262.4 100.8 all-gather.4
  381.7 226.3 reduce-scatter.1
